TPU v7x, 256 devices: a whole 4x4x8 slice. The times are simulated.
256 devices in a mesh: blk: 8 (over z), lat: 4 (over x), depth: 8 (over y, core).
Axes of the slice: x: 4, y: 4, z: 8, core: 2. Of those that a mesh axis runs over, the one named last changes fastest.
Arguments:
- face_len: int32 [8, 4, 8, 6], P('blk', 'lat', 'depth'), may hold values from 0 to 128, as said below
- residual: float32 [8, 4, 8, 768, 512], P('blk', 'lat', 'depth'), as said below
- prev_direction: float32 [8, 4, 8, 768, 512], P('blk', 'lat', 'depth'), as said below
- prev_rho: float32 [512], replicated, may hold values from 0.5 to 4
- schur: float32 [8, 4, 8, 768, 768], P('blk', 'lat', 'depth'), as said below
- neumann: float32 [8, 4, 8, 768, 768], P('blk', 'lat', 'depth'), as said below
- coarse_basis: float32 [8, 4, 8, 768, 256], P('blk', 'lat', 'depth'), may hold values from -0.21875 to 0.21875
- coarse_inverse: float32 [8, 4, 8, 256, 256], P('blk', 'lat', 'depth'), as said below
- prim_owner: int32 [8, 4, 8, 256, 1], P('blk', 'lat', 'depth'), may hold values from 0 to 31; in each aligned block of 256 rows (0 to 255, 256 to 511, ..., all dimensions but the last counted through in order) at most 24 rows name the same one
- coarse_row: int32 [8, 4, 8, 256], P('blk', 'lat', 'depth'), may hold values from 0 to 255
Outputs:
- new_residual: float32 [8, 4, 8, 768, 512], P('blk', 'lat', 'depth')
- direction: float32 [8, 4, 8, 768, 512], P('blk', 'lat', 'depth')
- rho_now: float32 [512], replicated
- step_alpha: float32 [512], replicated
- res_norm: float32 [512], replicated
Inputs may be any that keep to these rules, and one draw needn't show every extreme that they name: `face_len`: two subdomains that share a face have equal lengths on it; faces on the outer ends of lat and depth have length 0. `residual`: the two copies of a shared interface row are equal, and rows past a face's length are zero. `prev_direction`: the two copies of a shared interface row are equal, and rows past a face's length are zero. `schur`: each matrix has a positive definite symmetric part. `neumann`: each matrix has a positive definite symmetric part. `coarse_inverse`: each matrix has a positive definite symmetric part. `prim_owner`: at most 24 primal dofs of one subdomain have the same owner.
All inputs are finite; a program needn't handle non-finite values.
Results may differ from a plain program's by a relative error of at most 0.00005.
Values sent between devices are 32-bit elements; how exact they have to be, the bound alone decides.
A program may use at most 64 MiB of HBM per device.

v0:
```python
import jax
import jax.numpy as jnp
from jax import lax
from jax.sharding import PartitionSpec as P

CAP = 24
exact_mode = lax.Precision.HIGHEST


def from_behind(x, axis, by):
    devices = lax.axis_size(axis)
    return lax.ppermute(x, axis, [(i, (i + by) % devices) for i in range(devices)])


def passed_along(block, axis, distance):
    devices = range(lax.axis_size(axis))
    route = [(i - distance, i) for i in devices if i - distance in devices]
    return lax.ppermute(block, axis, route)


def product(left, right):
    return jnp.dot(left, right, precision=exact_mode, preferred_element_type=jnp.float32)


def product_t(left, right):
    return lax.dot_general(
        left,
        right,
        (((0,), (0,)), ((), ())),
        precision=exact_mode,
        preferred_element_type=jnp.float32,
    )


def assemble(vector, live_mask):
    col_count = vector.shape[1]
    face_rows = vector.shape[0] // 6
    face_list = vector.reshape(6, face_rows, col_count)
    received = [None] * 6
    for facing in range(2):
        shift_by = 1 - 2 * facing
        received[facing] = from_behind(face_list[1 - facing], "blk", shift_by)
        received[2 + facing] = passed_along(face_list[3 - facing], "lat", shift_by)
        received[4 + facing] = passed_along(face_list[5 - facing], "depth", shift_by)
    return live_mask * (vector + jnp.stack(received).reshape(vector.shape))


def coarse_level(coarse_terms, owner_ids, row_ids, inverse):
    primal, col_count = coarse_terms.shape
    owners = lax.axis_size(("blk", "lat"))
    slots = owners * CAP
    owner_hit = (owner_ids[:, None] == lax.broadcasted_iota(jnp.int32, (primal, owners), 1)).astype(
        jnp.int32
    )
    owner_rank = jnp.sum(jnp.cumsum(owner_hit, axis=0) * owner_hit, axis=1) - 1
    slot_index = owner_ids * CAP + owner_rank
    packer = slot_index[None, :] == lax.broadcasted_iota(jnp.int32, (slots, primal), 0)
    pack_table = packer.astype(jnp.float32)
    outgoing = product(pack_table, coarse_terms).reshape(owners, CAP, col_count)
    outgoing_rows = (jnp.sum(jnp.where(packer, row_ids[None, :] + 1, 0), axis=1) - 1).reshape(
        owners, CAP
    )
    incoming, incoming_rows = (
        lax.all_to_all(outgoing, ("blk", "lat"), split_axis=0, concat_axis=0, tiled=True),
        lax.all_to_all(outgoing_rows, ("blk", "lat"), split_axis=0, concat_axis=0, tiled=True),
    )
    owned_rows = inverse.shape[0]
    picker = (
        incoming_rows.reshape(1, slots) == lax.broadcasted_iota(jnp.int32, (owned_rows, slots), 0)
    ).astype(jnp.float32)
    gathered = product(picker, incoming.reshape(slots, col_count))
    solved = product(inverse, gathered)
    answers = product_t(picker, solved)
    returned = lax.all_to_all(
        answers.reshape(owners, CAP, col_count),
        ("blk", "lat"),
        split_axis=0,
        concat_axis=0,
        tiled=True,
    )
    return product_t(pack_table, returned.reshape(slots, col_count))


def shards(
    face_len,
    residual,
    prev_direction,
    prev_rho,
    schur,
    neumann,
    coarse_basis,
    coarse_inverse,
    prim_owner,
    coarse_row,
):
    row_count = residual.shape[3]
    col_count = residual.shape[4]
    face_rows = row_count // 6
    primal = coarse_basis.shape[4]
    owned_rows = coarse_inverse.shape[3]
    lengths = face_len.reshape(6)
    live_mask = (
        (lax.broadcasted_iota(jnp.int32, (6, face_rows), 1) < lengths[:, None])
        .astype(jnp.float32)
        .reshape(row_count, 1)
    )
    residual_live = live_mask * residual.reshape(row_count, col_count)
    weighted = 0.5 * residual_live
    local_part = product(neumann.reshape(row_count, row_count), weighted)
    basis = coarse_basis.reshape(row_count, primal)
    coarse_terms = product_t(basis, weighted)
    correction = coarse_level(
        coarse_terms,
        prim_owner.reshape(primal),
        coarse_row.reshape(primal),
        coarse_inverse.reshape(owned_rows, owned_rows),
    )
    precond_image = local_part + product(basis, correction)
    precond = 0.5 * assemble(precond_image, live_mask)
    devices = lax.axis_size(("blk", "lat", "depth"))
    norm_scale = 0.5 / (devices * row_count)
    rho_now = norm_scale * lax.psum(
        jnp.sum(residual_live * precond, axis=0), ("blk", "lat", "depth")
    )
    direction = precond + rho_now / prev_rho * (
        live_mask * prev_direction.reshape(row_count, col_count)
    )
    schur_image = product(schur.reshape(row_count, row_count), direction)
    applied = assemble(schur_image, live_mask)
    curv_sum = lax.psum(jnp.sum(direction * applied, axis=0), ("blk", "lat", "depth"))
    step_alpha = rho_now / (norm_scale * curv_sum)
    new_residual = residual_live - step_alpha * applied
    res_norm = norm_scale * lax.psum(
        jnp.sum(new_residual * new_residual, axis=0), ("blk", "lat", "depth")
    )
    out_shape = (1, 1, 1, row_count, col_count)
    return (
        new_residual.reshape(out_shape),
        direction.reshape(out_shape),
        rho_now,
        step_alpha,
        res_norm,
    )


def solution(mesh):
    in_specs = (
        P("blk", "lat", "depth", None),
        P("blk", "lat", "depth", None, None),
        P("blk", "lat", "depth", None, None),
        P(),
        P("blk", "lat", "depth", None, None),
        P("blk", "lat", "depth", None, None),
        P("blk", "lat", "depth", None, None),
        P("blk", "lat", "depth", None, None),
        P("blk", "lat", "depth", None, None),
        P("blk", "lat", "depth", None),
    )
    out_specs = (
        P("blk", "lat", "depth", None, None),
        P("blk", "lat", "depth", None, None),
        P(),
        P(),
        P(),
    )
    return jax.shard_map(shards, mesh=mesh, in_specs=in_specs, out_specs=out_specs, check_vma=False)
```

profile of v0, /device:TPU:1, one launch (start us, length us, event | category | flops | bytes accessed | tf_op | source)
XLA Modules:
  0.0 437.7 jit_solution(7040188213010964891)
XLA Ops:
  5.3 11.9 %all-to-all-start = ((s32[32,1,24]{2,1,0:T(1,128)}), s32[32,1,24]{2,1,0:T(1,128)S(1)}, u32[]{:S(2)}, u32[]{:S(2)}) async-start(s32[32,1,24]{2,1,0:T(1,128)} %bitcast.9), calls=%async_computation | async-start | bytes 32768 | tf_op jit(solution)/shard_map/all_to_all | solution.py:65
  17.9 4.4 %fusion.6 = f32[512,256]{1,0:T(8,128)S(1)} fusion(f32[1,1,1,768,512]{4,3,2,1,0:T(8,128)} %param.11, f32[1,1,1,768,256]{4,3,2,1,0:T(8,128)} %param.16, f32[768]{0:T(1024)S(1)} %convert_bitcast_fusion), kind=kOutput, calls=%fused_computation.7 | convolution fusion | flops 1208745984 | bytes 2886656 | tf_op jit(solution)/shard_map/dot_general | solution.py:26
  22.3 2.0 fusion.17
  24.3 1.4 all-to-all-done
  25.7 7.9 %all-to-all-start.1 = ((f32[32,24,512]{2,1,0:T(8,128)}), f32[32,24,512]{2,1,0:T(8,128)}, u32[]{:S(2)}, u32[]{:S(2)}) async-start(f32[32,24,512]{2,1,0:T(8,128)} %bitcast.103), calls=%async_computation.1 | async-start | bytes 3145728 | tf_op jit(solution)/shard_map/all_to_all | solution.py:64
  34.9 35.1 %all-to-all-done.1 = f32[32,24,512]{2,1,0:T(8,128)} async-done(((f32[32,24,512]{2,1,0:T(8,128)}), f32[32,24,512]{2,1,0:T(8,128)}, u32[]{:S(2)}, u32[]{:S(2)}) %all-to-all-start.1) | async-done | bytes 1572896 | tf_op jit(solution)/shard_map/all_to_all | solution.py:64
  70.1 2.4 fusion.15
  73.5 2.1 fusion.22
  75.6 7.3 %all-to-all-start.2 = ((f32[32,24,512]{2,1,0:T(8,128)}), f32[32,24,512]{2,1,0:T(8,128)}, u32[]{:S(2)}, u32[]{:S(2)}) async-start(f32[32,24,512]{2,1,0:T(8,128)} %bitcast.100), calls=%async_computation.2 | async-start | bytes 3145728 | tf_op jit(solution)/shard_map/all_to_all | solution.py:74
  82.9 10.3 %fusion.2 = f32[512,768]{1,0:T(8,128)} fusion(f32[1,1,1,768,768]{4,3,2,1,0:T(8,128)S(1)} %copy-done, f32[1,1,1,768,512]{4,3,2,1,0:T(8,128)} %param.11, f32[768]{0:T(1024)S(1)} %convert_bitcast_fusion), kind=kOutput, calls=%fused_computation.2 | convolution fusion | flops 3624665088 | bytes 5508096 | tf_op jit(solution)/shard_map/dot_general | solution.py:22
  93.2 25.3 %all-to-all-done.2 = f32[32,24,512]{2,1,0:T(8,128)} async-done(((f32[32,24,512]{2,1,0:T(8,128)}), f32[32,24,512]{2,1,0:T(8,128)}, u32[]{:S(2)}, u32[]{:S(2)}) %all-to-all-start.2) | async-done | bytes 1572896 | tf_op jit(solution)/shard_map/all_to_all | solution.py:74
  118.5 2.5 fusion.16
  121.1 2.6 add_bitcast_fusion
  123.7 1.0 fusion.37
  125.8 2.0 collective-permute-start.1
  127.7 3.0 copy.40
  130.7 3.0 copy.45
  133.8 5.3 %collective-permute-start.2 = (f32[128,512]{0,1:T(8,128)S(1)}, f32[128,512]{0,1:T(8,128)S(1)}, u32[]{:S(2)}, u32[]{:S(2)}) collective-permute-start(f32[128,512]{0,1:T(8,128)S(1)} %get-tuple-element.38), channel_id=1, source_target_pairs={{0,8},{8,16},{16,24},{1,9},{9,17},{17,25},{2,10},{10,18},{18,26},{... | collective-permute-start | bytes 786440 | tf_op jit(solution)/shard_map/ppermute | solution.py:18
  139.1 1.3 collective-permute-start.3
  140.4 5.9 %collective-permute-start.4 = (f32[128,512]{0,1:T(8,128)S(1)}, f32[128,512]{0,1:T(8,128)S(1)}, u32[]{:S(2)}, u32[]{:S(2)}) collective-permute-start(f32[128,512]{0,1:T(8,128)S(1)} %get-tuple-element.36), channel_id=1, source_target_pairs={{0,1},{1,2},{2,3},{3,4},{4,5},{5,6},{6,7},{8,9},{9,10},{10,11},{11... | collective-permute-start | bytes 786440 | tf_op jit(solution)/shard_map/ppermute | solution.py:18
  146.4 1.9 collective-permute-start.5
  148.3 1.7 bitcast_dynamic-update-slice_fusion.11
  150.0 1.7 bitcast_dynamic-update-slice_fusion.10
  154.8 3.0 copy.43
  157.8 3.0 copy.44
  160.8 2.7 multiply_reduce_fusion.2
  163.6 75.6 %psum.21 = f32[512]{0:T(512)S(1)} all-reduce(f32[512]{0:T(512)S(1)} %multiply_reduce_fusion.2), channel_id=1, replica_groups=mesh['blk'=8,'lat'=4,'depth'=8] {'blk','lat','depth'}, use_global_device_ids=true, to_apply=%region_5.6 | all-reduce | flops 512 | bytes 4096 | tf_op jit(solution)/shard_map/psum | solution.py:122
  239.2 2.9 fusion.5
  242.3 4.0 fusion.9
  246.4 1.0 fusion.36
  247.7 1.8 collective-permute-start.6
  250.4 2.9 collective-permute-start.8
  253.3 1.3 collective-permute-start.9
  254.6 2.6 collective-permute-start.10
  257.2 3.0 copy.49
  260.2 3.0 collective-permute-start.11
  263.3 1.7 bitcast_dynamic-update-slice_fusion.5
  265.0 1.7 bitcast_dynamic-update-slice_fusion.4
  266.7 1.7 bitcast_dynamic-update-slice_fusion.3
  268.3 1.7 bitcast_dynamic-update-slice_fusion.2
  270.0 1.7 bitcast_dynamic-update-slice_fusion.1
  272.4 3.1 copy.46
  275.4 3.0 copy.47
  278.5 2.6 multiply_reduce_fusion.1
  281.1 74.9 %psum.22 = f32[512]{0:T(512)S(1)} all-reduce(f32[512]{0:T(512)S(1)} %multiply_reduce_fusion.1), channel_id=1, replica_groups=mesh['blk'=8,'lat'=4,'depth'=8] {'blk','lat','depth'}, use_global_device_ids=true, to_apply=%region_7.8 | all-reduce | flops 512 | bytes 4096 | tf_op jit(solution)/shard_map/psum | solution.py:130
  356.0 3.9 multiply_reduce_fusion
  359.9 3.0 copy.48
  362.9 74.2 %psum.23 = f32[512]{0:T(512)S(1)} all-reduce(f32[512]{0:T(512)S(1)} %get-tuple-element.25), channel_id=1, replica_groups=mesh['blk'=8,'lat'=4,'depth'=8] {'blk','lat','depth'}, use_global_device_ids=true, to_apply=%region_9.10 | all-reduce | flops 512 | bytes 4096 | tf_op jit(solution)/shard_map/psum | solution.py:133
  (60 shorter events, 14.6 us)
Async XLA Ops:
  0.6 82.2 %copy-start = (f32[1,1,1,768,768]{4,3,2,1,0:T(8,128)S(1)}, f32[1,1,1,768,768]{4,3,2,1,0:T(8,128)}, u32[]{:S(2)}) copy-start(f32[1,1,1,768,768]{4,3,2,1,0:T(8,128)} %param.15) | copy-start | bytes 7077892
  5.3 20.4 %all-to-all-start = ((s32[32,1,24]{2,1,0:T(1,128)}), s32[32,1,24]{2,1,0:T(1,128)S(1)}, u32[]{:S(2)}, u32[]{:S(2)}) async-start(s32[32,1,24]{2,1,0:T(1,128)} %bitcast.9), calls=%async_computation | async-start | bytes 32768 | tf_op jit(solution)/shard_map/all_to_all | solution.py:65
  25.7 44.4 %all-to-all-start.1 = ((f32[32,24,512]{2,1,0:T(8,128)}), f32[32,24,512]{2,1,0:T(8,128)}, u32[]{:S(2)}, u32[]{:S(2)}) async-start(f32[32,24,512]{2,1,0:T(8,128)} %bitcast.103), calls=%async_computation.1 | async-start | bytes 3145728 | tf_op jit(solution)/shard_map/all_to_all | solution.py:64
  33.6 38.8 %copy-start.7 = (f32[1,1,1,256,256]{4,3,2,1,0:T(8,128)S(1)}, f32[1,1,1,256,256]{4,3,2,1,0:T(8,128)}, u32[]{:S(2)}) copy-start(f32[1,1,1,256,256]{4,3,2,1,0:T(8,128)} %param.17) | copy-start | bytes 786436
  75.6 42.9 %all-to-all-start.2 = ((f32[32,24,512]{2,1,0:T(8,128)}), f32[32,24,512]{2,1,0:T(8,128)}, u32[]{:S(2)}, u32[]{:S(2)}) async-start(f32[32,24,512]{2,1,0:T(8,128)} %bitcast.100), calls=%async_computation.2 | async-start | bytes 3145728 | tf_op jit(solution)/shard_map/all_to_all | solution.py:74
  82.9 38.2 %copy-start.5 = (f32[1,1,1,768,256]{4,3,2,1,0:T(8,128)S(1)}, f32[1,1,1,768,256]{4,3,2,1,0:T(8,128)}, u32[]{:S(2)}) copy-start(f32[1,1,1,768,256]{4,3,2,1,0:T(8,128)} %param.16) | copy-start | bytes 2359300
  118.5 2.6 copy-start.4
  123.7 1.3 copy-start.2
  125.0 21.3 %collective-permute-start = (f32[128,512]{0,1:T(8,128)}, f32[128,512]{0,1:T(8,128)}, u32[]{:S(2)}, u32[]{:S(2)}) collective-permute-start(f32[128,512]{0,1:T(8,128)} %get-tuple-element.40), channel_id=1, source_target_pairs={{0,32},{32,64},{64,96},{96,128},{128,160},{160,192},{192,224},{224... | collective-permute-start | bytes 786440 | tf_op jit(solution)/shard_map/ppermute | solution.py:12
  125.8 24.2 %collective-permute-start.1 = (f32[128,512]{0,1:T(8,128)}, f32[128,512]{0,1:T(8,128)}, u32[]{:S(2)}, u32[]{:S(2)}) collective-permute-start(f32[128,512]{0,1:T(8,128)} %get-tuple-element.39), channel_id=1, source_target_pairs={{0,224},{32,0},{64,32},{96,64},{128,96},{160,128},{192,160},{224,1... | collective-permute-start | bytes 786440 | tf_op jit(solution)/shard_map/ppermute | solution.py:12
  133.8 17.9 %collective-permute-start.2 = (f32[128,512]{0,1:T(8,128)S(1)}, f32[128,512]{0,1:T(8,128)S(1)}, u32[]{:S(2)}, u32[]{:S(2)}) collective-permute-start(f32[128,512]{0,1:T(8,128)S(1)} %get-tuple-element.38), channel_id=1, source_target_pairs={{0,8},{8,16},{16,24},{1,9},{9,17},{17,25},{2,10},{10,18},{18,26},{... | collective-permute-start | bytes 786440 | tf_op jit(solution)/shard_map/ppermute | solution.py:18
  139.1 13.3 %collective-permute-start.3 = (f32[128,512]{0,1:T(8,128)S(1)}, f32[128,512]{0,1:T(8,128)S(1)}, u32[]{:S(2)}, u32[]{:S(2)}) collective-permute-start(f32[128,512]{0,1:T(8,128)S(1)} %get-tuple-element.37), channel_id=1, source_target_pairs={{8,0},{16,8},{24,16},{9,1},{17,9},{25,17},{10,2},{18,10},{26,18},{... | collective-permute-start | bytes 786440 | tf_op jit(solution)/shard_map/ppermute | solution.py:18
  140.4 12.7 %collective-permute-start.4 = (f32[128,512]{0,1:T(8,128)S(1)}, f32[128,512]{0,1:T(8,128)S(1)}, u32[]{:S(2)}, u32[]{:S(2)}) collective-permute-start(f32[128,512]{0,1:T(8,128)S(1)} %get-tuple-element.36), channel_id=1, source_target_pairs={{0,1},{1,2},{2,3},{3,4},{4,5},{5,6},{6,7},{8,9},{9,10},{10,11},{11... | collective-permute-start | bytes 786440 | tf_op jit(solution)/shard_map/ppermute | solution.py:18
  146.4 7.7 %collective-permute-start.5 = (f32[128,512]{0,1:T(8,128)S(1)}, f32[128,512]{0,1:T(8,128)S(1)}, u32[]{:S(2)}, u32[]{:S(2)}) collective-permute-start(f32[128,512]{0,1:T(8,128)S(1)} %get-tuple-element.35), channel_id=1, source_target_pairs={{1,0},{2,1},{3,2},{4,3},{5,4},{6,5},{7,6},{9,8},{10,9},{11,10},{12... | collective-permute-start | bytes 786440 | tf_op jit(solution)/shard_map/ppermute | solution.py:18
  160.8 78.4 %copy-start.10 = (f32[512]{0:T(512)S(1)}, f32[512]{0:T(512)}, u32[]{:S(2)}) copy-start(f32[512]{0:T(512)} %param.13) | copy-start | bytes 6148
  239.2 116.8 %copy-start.9 = (f32[512]{0:T(512)}, f32[512]{0:T(512)S(1)}, u32[]{:S(2)}) copy-start(f32[512]{0:T(512)S(1)} %get-tuple-element.28) | copy-start | bytes 6148
  239.2 3.1 copy-start.6
  242.3 4.1 copy-start.3
  246.4 1.3 copy-start.1
  247.7 12.6 %collective-permute-start.6 = (f32[128,512]{0,1:T(8,128)}, f32[128,512]{0,1:T(8,128)}, u32[]{:S(2)}, u32[]{:S(2)}) collective-permute-start(f32[128,512]{0,1:T(8,128)} %get-tuple-element.34), channel_id=1, source_target_pairs={{0,32},{32,64},{64,96},{96,128},{128,160},{160,192},{192,224},{224... | collective-permute-start | bytes 786440 | tf_op jit(solution)/shard_map/ppermute | solution.py:12
  249.5 15.5 %collective-permute-start.7 = (f32[128,512]{0,1:T(8,128)}, f32[128,512]{0,1:T(8,128)}, u32[]{:S(2)}, u32[]{:S(2)}) collective-permute-start(f32[128,512]{0,1:T(8,128)} %get-tuple-element.33), channel_id=1, source_target_pairs={{0,224},{32,0},{64,32},{96,64},{128,96},{160,128},{192,160},{224,1... | collective-permute-start | bytes 786440 | tf_op jit(solution)/shard_map/ppermute | solution.py:12
  250.4 16.3 %collective-permute-start.8 = (f32[128,512]{0,1:T(8,128)S(1)}, f32[128,512]{0,1:T(8,128)}, u32[]{:S(2)}, u32[]{:S(2)}) collective-permute-start(f32[128,512]{0,1:T(8,128)S(1)} %get-tuple-element.32), channel_id=1, source_target_pairs={{0,8},{8,16},{16,24},{1,9},{9,17},{17,25},{2,10},{10,18},{18,26},{... | collective-permute-start | bytes 786440 | tf_op jit(solution)/shard_map/ppermute | solution.py:18
  253.3 15.0 %collective-permute-start.9 = (f32[128,512]{0,1:T(8,128)S(1)}, f32[128,512]{0,1:T(8,128)}, u32[]{:S(2)}, u32[]{:S(2)}) collective-permute-start(f32[128,512]{0,1:T(8,128)S(1)} %get-tuple-element.31), channel_id=1, source_target_pairs={{8,0},{16,8},{24,16},{9,1},{17,9},{25,17},{10,2},{18,10},{26,18},{... | collective-permute-start | bytes 786440 | tf_op jit(solution)/shard_map/ppermute | solution.py:18
  254.6 15.4 %collective-permute-start.10 = (f32[128,512]{0,1:T(8,128)S(1)}, f32[128,512]{0,1:T(8,128)}, u32[]{:S(2)}, u32[]{:S(2)}) collective-permute-start(f32[128,512]{0,1:T(8,128)S(1)} %get-tuple-element.30), channel_id=1, source_target_pairs={{0,1},{1,2},{2,3},{3,4},{4,5},{5,6},{6,7},{8,9},{9,10},{10,11},{11... | collective-permute-start | bytes 786440 | tf_op jit(solution)/shard_map/ppermute | solution.py:18
  260.2 11.4 %collective-permute-start.11 = (f32[128,512]{0,1:T(8,128)S(1)}, f32[128,512]{0,1:T(8,128)S(1)}, u32[]{:S(2)}, u32[]{:S(2)}) collective-permute-start(f32[128,512]{0,1:T(8,128)S(1)} %get-tuple-element.29), channel_id=1, source_target_pairs={{1,0},{2,1},{3,2},{4,3},{5,4},{6,5},{7,6},{9,8},{10,9},{11,10},{12... | collective-permute-start | bytes 786440 | tf_op jit(solution)/shard_map/ppermute | solution.py:18
  356.0 3.9 copy-start.8
where the time goes:
time: 439 us; the launch traced here: 438 us
  blocking collectives  225 us (51%)
  waiting for transfers between devices  62.1 us (14%)
  starting transfers between devices  56.7 us (13%)
  local copies, waits for them, and re-layouts  43.9 us (10%)
  matrix products  31.4 us (7%)
  other arithmetic  18 us (4%)
    psum x1, blocking collectives, shards(): lax.psum(jnp.sum(residual_live * precond, axis=0), ('blk', 'lat', 'depth'))  75.6 us
    psum x1, blocking collectives, shards(): lax.psum(jnp.sum(direction * applied, axis=0), ('blk', 'lat', 'depth'))  74.9 us
    psum x1, blocking collectives, shards(): lax.psum(jnp.sum(new_residual * new_residual, axis=0), ('blk', 'lat', 'de...  74.2 us
    all_to_all x1, waiting for transfers between devices, coarse_level(): lax.all_to_all(outgoing, ('blk', 'lat'), split_axis=0, concat_axis=0, til...  35.1 us
    unnamed x36, local copies, waits for them, and re-layouts  26.8 us
    all_to_all x1, waiting for transfers between devices, coarse_level(): lax.all_to_all(answers.reshape(owners, CAP, col_count), ('blk', 'lat'), s...  25.3 us
    ppermute x8, starting transfers between devices, passed_along(): return lax.ppermute(block, axis, route)  24.4 us
    dot_general x6, matrix products, product(): jnp.dot(left, right, precision=exact_mode, preferred_element_type=jnp.flo...  22.3 us
  transfers between devices with their start and end apart: 15, of which 4 were waited for; matrix products, arithmetic and copies ran while one was open for 10% of the time, Pallas kernels for 0%

commit v1 on v0

--- a/solution.py
+++ b/solution.py
@@ -127,7 +127,9 @@
     )
     schur_image = product(schur.reshape(row_count, row_count), direction)
     applied = assemble(schur_image, live_mask)
-    curv_sum = lax.psum(jnp.sum(direction * applied, axis=0), ("blk", "lat", "depth"))
+    curv_sum = lax.all_gather(jnp.sum(direction * applied, axis=0), ("blk", "lat", "depth")).sum(
+        axis=0
+    )
     step_alpha = rho_now / (norm_scale * curv_sum)
     new_residual = residual_live - step_alpha * applied
     res_norm = norm_scale * lax.psum(

time: 439 us -> 439 us (level); the launches traced: 438 us -> 431 us
  blocking collectives: 225 us -> 217 us
    psum x1 -> x0, blocking collectives: 74.9 us -> none  [shards(): lax.psum(jnp.sum(direction * applied, axis=0), ('blk', 'lat', 'depth'))]
    all_gather x0 -> x1, blocking collectives: none -> 68 us  [shards(): lax.all_gather(jnp.sum(direction * applied, axis=0), ('blk', 'lat', 'dept...]
where the time goes in v1:
time: 439 us; the launch traced here: 431 us
  blocking collectives  217 us (49%)
  waiting for transfers between devices  62.3 us (14%)
  starting transfers between devices  57.2 us (13%)
  local copies, waits for them, and re-layouts  43.9 us (10%)
  matrix products  31.4 us (7%)
  other arithmetic  18.3 us (4%)
    psum x1, blocking collectives, shards(): lax.psum(jnp.sum(residual_live * precond, axis=0), ('blk', 'lat', 'depth'))  75.6 us
    psum x1, blocking collectives, shards(): lax.psum(jnp.sum(new_residual * new_residual, axis=0), ('blk', 'lat', 'de...  73.3 us
    all_gather x1, blocking collectives, shards(): lax.all_gather(jnp.sum(direction * applied, axis=0), ('blk', 'lat', 'dept...  68 us
    all_to_all x1, waiting for transfers between devices, coarse_level(): lax.all_to_all(outgoing, ('blk', 'lat'), split_axis=0, concat_axis=0, til...  35.1 us
    unnamed x36, local copies, waits for them, and re-layouts  26.8 us
    all_to_all x1, waiting for transfers between devices, coarse_level(): lax.all_to_all(answers.reshape(owners, CAP, col_count), ('blk', 'lat'), s...  25.5 us
    ppermute x8, starting transfers between devices, passed_along(): return lax.ppermute(block, axis, route)  24.3 us
    dot_general x6, matrix products, product(): jnp.dot(left, right, precision=exact_mode, preferred_element_type=jnp.flo...  22.3 us
  transfers between devices with their start and end apart: 15, of which 4 were waited for; matrix products, arithmetic and copies ran while one was open for 10% of the time, Pallas kernels for 0%

profile of v1, /device:TPU:1, one launch (start us, length us, event | category | flops | bytes accessed | tf_op | source)
XLA Modules:
  0.0 431.1 jit_solution(1173386846563768257)
XLA Ops:
  5.3 11.9 %all-to-all-start = ((s32[32,1,24]{2,1,0:T(1,128)}), s32[32,1,24]{2,1,0:T(1,128)S(1)}, u32[]{:S(2)}, u32[]{:S(2)}) async-start(s32[32,1,24]{2,1,0:T(1,128)} %bitcast.9), calls=%async_computation | async-start | bytes 32768 | tf_op jit(solution)/shard_map/all_to_all | solution.py:65
  17.9 4.4 %fusion.6 = f32[512,256]{1,0:T(8,128)S(1)} fusion(f32[1,1,1,768,512]{4,3,2,1,0:T(8,128)} %param.11, f32[1,1,1,768,256]{4,3,2,1,0:T(8,128)} %param.16, f32[768]{0:T(1024)S(1)} %convert_bitcast_fusion), kind=kOutput, calls=%fused_computation.7 | convolution fusion | flops 1208745984 | bytes 2886656 | tf_op jit(solution)/shard_map/dot_general | solution.py:26
  22.3 2.0 fusion.17
  24.3 1.4 all-to-all-done
  25.7 7.9 %all-to-all-start.1 = ((f32[32,24,512]{2,1,0:T(8,128)}), f32[32,24,512]{2,1,0:T(8,128)}, u32[]{:S(2)}, u32[]{:S(2)}) async-start(f32[32,24,512]{2,1,0:T(8,128)} %bitcast.104), calls=%async_computation.1 | async-start | bytes 3145728 | tf_op jit(solution)/shard_map/all_to_all | solution.py:64
  34.9 35.1 %all-to-all-done.1 = f32[32,24,512]{2,1,0:T(8,128)} async-done(((f32[32,24,512]{2,1,0:T(8,128)}), f32[32,24,512]{2,1,0:T(8,128)}, u32[]{:S(2)}, u32[]{:S(2)}) %all-to-all-start.1) | async-done | bytes 1572896 | tf_op jit(solution)/shard_map/all_to_all | solution.py:64
  70.1 2.4 fusion.15
  73.5 2.1 fusion.22
  75.6 7.6 %all-to-all-start.2 = ((f32[32,24,512]{2,1,0:T(8,128)}), f32[32,24,512]{2,1,0:T(8,128)}, u32[]{:S(2)}, u32[]{:S(2)}) async-start(f32[32,24,512]{2,1,0:T(8,128)} %bitcast.101), calls=%async_computation.2 | async-start | bytes 3145728 | tf_op jit(solution)/shard_map/all_to_all | solution.py:74
  83.2 10.3 %fusion.2 = f32[512,768]{1,0:T(8,128)} fusion(f32[1,1,1,768,768]{4,3,2,1,0:T(8,128)S(1)} %copy-done, f32[1,1,1,768,512]{4,3,2,1,0:T(8,128)} %param.11, f32[768]{0:T(1024)S(1)} %convert_bitcast_fusion), kind=kOutput, calls=%fused_computation.2 | convolution fusion | flops 3624665088 | bytes 5508096 | tf_op jit(solution)/shard_map/dot_general | solution.py:22
  93.5 25.5 %all-to-all-done.2 = f32[32,24,512]{2,1,0:T(8,128)} async-done(((f32[32,24,512]{2,1,0:T(8,128)}), f32[32,24,512]{2,1,0:T(8,128)}, u32[]{:S(2)}, u32[]{:S(2)}) %all-to-all-start.2) | async-done | bytes 1572896 | tf_op jit(solution)/shard_map/all_to_all | solution.py:74
  118.9 2.5 fusion.16
  121.5 2.6 add_bitcast_fusion
  124.1 1.0 fusion.37
  126.3 2.0 collective-permute-start.1
  128.3 3.0 copy.40
  131.3 3.0 copy.45
  134.3 5.4 %collective-permute-start.2 = (f32[128,512]{0,1:T(8,128)S(1)}, f32[128,512]{0,1:T(8,128)S(1)}, u32[]{:S(2)}, u32[]{:S(2)}) collective-permute-start(f32[128,512]{0,1:T(8,128)S(1)} %get-tuple-element.38), channel_id=1, source_target_pairs={{0,8},{8,16},{16,24},{1,9},{9,17},{17,25},{2,10},{10,18},{18,26},{... | collective-permute-start | bytes 786440 | tf_op jit(solution)/shard_map/ppermute | solution.py:18
  139.7 1.3 collective-permute-start.3
  141.0 5.9 %collective-permute-start.4 = (f32[128,512]{0,1:T(8,128)S(1)}, f32[128,512]{0,1:T(8,128)S(1)}, u32[]{:S(2)}, u32[]{:S(2)}) collective-permute-start(f32[128,512]{0,1:T(8,128)S(1)} %get-tuple-element.36), channel_id=1, source_target_pairs={{0,1},{1,2},{2,3},{3,4},{4,5},{5,6},{6,7},{8,9},{9,10},{10,11},{11... | collective-permute-start | bytes 786440 | tf_op jit(solution)/shard_map/ppermute | solution.py:18
  147.0 1.9 collective-permute-start.5
  148.9 1.7 bitcast_dynamic-update-slice_fusion.11
  150.6 1.7 bitcast_dynamic-update-slice_fusion.10
  155.4 3.0 copy.43
  158.4 3.0 copy.44
  161.4 2.7 multiply_reduce_fusion.2
  164.2 75.6 %psum.14 = f32[512]{0:T(512)S(1)} all-reduce(f32[512]{0:T(512)S(1)} %multiply_reduce_fusion.2), channel_id=1, replica_groups=mesh['blk'=8,'lat'=4,'depth'=8] {'blk','lat','depth'}, use_global_device_ids=true, to_apply=%region_5.6 | all-reduce | flops 512 | bytes 4096 | tf_op jit(solution)/shard_map/psum | solution.py:122
  239.8 2.9 fusion.5
  242.9 4.0 fusion.9
  247.0 1.0 fusion.36
  248.3 1.8 collective-permute-start.6
  251.0 2.9 collective-permute-start.8
  253.9 1.3 collective-permute-start.9
  255.2 2.6 collective-permute-start.10
  257.8 3.0 copy.49
  260.9 3.0 collective-permute-start.11
  263.9 1.7 bitcast_dynamic-update-slice_fusion.5
  265.6 1.7 bitcast_dynamic-update-slice_fusion.4
  267.2 1.7 bitcast_dynamic-update-slice_fusion.3
  268.9 1.7 bitcast_dynamic-update-slice_fusion.2
  270.6 1.7 bitcast_dynamic-update-slice_fusion.1
  273.0 3.1 copy.46
  276.0 3.0 copy.47
  279.0 2.6 multiply_reduce_fusion.1
  281.7 68.0 %all-gather.1 = f32[256,1,512]{2,1,0:T(1,128)S(1)} all-gather(f32[1,1,512]{2,1,0:T(1,128)S(1)} %bitcast.109), channel_id=2, replica_groups=mesh['blk'=8,'lat'=4,'depth'=8] {'blk','lat','depth'}, dimensions={0}, use_global_device_ids=true | all-gather | bytes 526336 | tf_op jit(solution)/shard_map/all_gather | solution.py:130
  350.1 3.9 multiply_reduce_fusion
  354.0 3.0 copy.48
  357.0 73.3 %psum.15 = f32[512]{0:T(512)S(1)} all-reduce(f32[512]{0:T(512)S(1)} %get-tuple-element.25), channel_id=1, replica_groups=mesh['blk'=8,'lat'=4,'depth'=8] {'blk','lat','depth'}, use_global_device_ids=true, to_apply=%region_9.10 | all-reduce | flops 512 | bytes 4096 | tf_op jit(solution)/shard_map/psum | solution.py:135
  (61 shorter events, 15.0 us)
Async XLA Ops:
  0.6 82.5 %copy-start = (f32[1,1,1,768,768]{4,3,2,1,0:T(8,128)S(1)}, f32[1,1,1,768,768]{4,3,2,1,0:T(8,128)}, u32[]{:S(2)}) copy-start(f32[1,1,1,768,768]{4,3,2,1,0:T(8,128)} %param.15) | copy-start | bytes 7077892
  5.3 20.4 %all-to-all-start = ((s32[32,1,24]{2,1,0:T(1,128)}), s32[32,1,24]{2,1,0:T(1,128)S(1)}, u32[]{:S(2)}, u32[]{:S(2)}) async-start(s32[32,1,24]{2,1,0:T(1,128)} %bitcast.9), calls=%async_computation | async-start | bytes 32768 | tf_op jit(solution)/shard_map/all_to_all | solution.py:65
  25.7 44.3 %all-to-all-start.1 = ((f32[32,24,512]{2,1,0:T(8,128)}), f32[32,24,512]{2,1,0:T(8,128)}, u32[]{:S(2)}, u32[]{:S(2)}) async-start(f32[32,24,512]{2,1,0:T(8,128)} %bitcast.104), calls=%async_computation.1 | async-start | bytes 3145728 | tf_op jit(solution)/shard_map/all_to_all | solution.py:64
  33.6 38.8 %copy-start.7 = (f32[1,1,1,256,256]{4,3,2,1,0:T(8,128)S(1)}, f32[1,1,1,256,256]{4,3,2,1,0:T(8,128)}, u32[]{:S(2)}) copy-start(f32[1,1,1,256,256]{4,3,2,1,0:T(8,128)} %param.17) | copy-start | bytes 786436
  75.6 43.4 %all-to-all-start.2 = ((f32[32,24,512]{2,1,0:T(8,128)}), f32[32,24,512]{2,1,0:T(8,128)}, u32[]{:S(2)}, u32[]{:S(2)}) async-start(f32[32,24,512]{2,1,0:T(8,128)} %bitcast.101), calls=%async_computation.2 | async-start | bytes 3145728 | tf_op jit(solution)/shard_map/all_to_all | solution.py:74
  83.2 38.3 %copy-start.5 = (f32[1,1,1,768,256]{4,3,2,1,0:T(8,128)S(1)}, f32[1,1,1,768,256]{4,3,2,1,0:T(8,128)}, u32[]{:S(2)}) copy-start(f32[1,1,1,768,256]{4,3,2,1,0:T(8,128)} %param.16) | copy-start | bytes 2359300
  118.9 2.6 copy-start.4
  124.1 1.3 copy-start.2
  125.5 21.5 %collective-permute-start = (f32[128,512]{0,1:T(8,128)}, f32[128,512]{0,1:T(8,128)}, u32[]{:S(2)}, u32[]{:S(2)}) collective-permute-start(f32[128,512]{0,1:T(8,128)} %get-tuple-element.40), channel_id=1, source_target_pairs={{0,32},{32,64},{64,96},{96,128},{128,160},{160,192},{192,224},{224... | collective-permute-start | bytes 786440 | tf_op jit(solution)/shard_map/ppermute | solution.py:12
  126.3 24.3 %collective-permute-start.1 = (f32[128,512]{0,1:T(8,128)}, f32[128,512]{0,1:T(8,128)}, u32[]{:S(2)}, u32[]{:S(2)}) collective-permute-start(f32[128,512]{0,1:T(8,128)} %get-tuple-element.39), channel_id=1, source_target_pairs={{0,224},{32,0},{64,32},{96,64},{128,96},{160,128},{192,160},{224,1... | collective-permute-start | bytes 786440 | tf_op jit(solution)/shard_map/ppermute | solution.py:12
  134.3 17.9 %collective-permute-start.2 = (f32[128,512]{0,1:T(8,128)S(1)}, f32[128,512]{0,1:T(8,128)S(1)}, u32[]{:S(2)}, u32[]{:S(2)}) collective-permute-start(f32[128,512]{0,1:T(8,128)S(1)} %get-tuple-element.38), channel_id=1, source_target_pairs={{0,8},{8,16},{16,24},{1,9},{9,17},{17,25},{2,10},{10,18},{18,26},{... | collective-permute-start | bytes 786440 | tf_op jit(solution)/shard_map/ppermute | solution.py:18
  139.7 13.3 %collective-permute-start.3 = (f32[128,512]{0,1:T(8,128)S(1)}, f32[128,512]{0,1:T(8,128)S(1)}, u32[]{:S(2)}, u32[]{:S(2)}) collective-permute-start(f32[128,512]{0,1:T(8,128)S(1)} %get-tuple-element.37), channel_id=1, source_target_pairs={{8,0},{16,8},{24,16},{9,1},{17,9},{25,17},{10,2},{18,10},{26,18},{... | collective-permute-start | bytes 786440 | tf_op jit(solution)/shard_map/ppermute | solution.py:18
  141.0 12.7 %collective-permute-start.4 = (f32[128,512]{0,1:T(8,128)S(1)}, f32[128,512]{0,1:T(8,128)S(1)}, u32[]{:S(2)}, u32[]{:S(2)}) collective-permute-start(f32[128,512]{0,1:T(8,128)S(1)} %get-tuple-element.36), channel_id=1, source_target_pairs={{0,1},{1,2},{2,3},{3,4},{4,5},{5,6},{6,7},{8,9},{9,10},{10,11},{11... | collective-permute-start | bytes 786440 | tf_op jit(solution)/shard_map/ppermute | solution.py:18
  147.0 7.7 %collective-permute-start.5 = (f32[128,512]{0,1:T(8,128)S(1)}, f32[128,512]{0,1:T(8,128)S(1)}, u32[]{:S(2)}, u32[]{:S(2)}) collective-permute-start(f32[128,512]{0,1:T(8,128)S(1)} %get-tuple-element.35), channel_id=1, source_target_pairs={{1,0},{2,1},{3,2},{4,3},{5,4},{6,5},{7,6},{9,8},{10,9},{11,10},{12... | collective-permute-start | bytes 786440 | tf_op jit(solution)/shard_map/ppermute | solution.py:18
  161.4 78.4 %copy-start.10 = (f32[512]{0:T(512)S(1)}, f32[512]{0:T(512)}, u32[]{:S(2)}) copy-start(f32[512]{0:T(512)} %param.13) | copy-start | bytes 6148
  239.8 110.2 %copy-start.9 = (f32[512]{0:T(512)}, f32[512]{0:T(512)S(1)}, u32[]{:S(2)}) copy-start(f32[512]{0:T(512)S(1)} %get-tuple-element.28) | copy-start | bytes 6148
  239.8 3.1 copy-start.6
  242.9 4.0 copy-start.3
  247.0 1.3 copy-start.1
  248.3 12.6 %collective-permute-start.6 = (f32[128,512]{0,1:T(8,128)}, f32[128,512]{0,1:T(8,128)}, u32[]{:S(2)}, u32[]{:S(2)}) collective-permute-start(f32[128,512]{0,1:T(8,128)} %get-tuple-element.34), channel_id=1, source_target_pairs={{0,32},{32,64},{64,96},{96,128},{128,160},{160,192},{192,224},{224... | collective-permute-start | bytes 786440 | tf_op jit(solution)/shard_map/ppermute | solution.py:12
  250.1 15.5 %collective-permute-start.7 = (f32[128,512]{0,1:T(8,128)}, f32[128,512]{0,1:T(8,128)}, u32[]{:S(2)}, u32[]{:S(2)}) collective-permute-start(f32[128,512]{0,1:T(8,128)} %get-tuple-element.33), channel_id=1, source_target_pairs={{0,224},{32,0},{64,32},{96,64},{128,96},{160,128},{192,160},{224,1... | collective-permute-start | bytes 786440 | tf_op jit(solution)/shard_map/ppermute | solution.py:12
  251.0 16.3 %collective-permute-start.8 = (f32[128,512]{0,1:T(8,128)S(1)}, f32[128,512]{0,1:T(8,128)}, u32[]{:S(2)}, u32[]{:S(2)}) collective-permute-start(f32[128,512]{0,1:T(8,128)S(1)} %get-tuple-element.32), channel_id=1, source_target_pairs={{0,8},{8,16},{16,24},{1,9},{9,17},{17,25},{2,10},{10,18},{18,26},{... | collective-permute-start | bytes 786440 | tf_op jit(solution)/shard_map/ppermute | solution.py:18
  253.9 15.0 %collective-permute-start.9 = (f32[128,512]{0,1:T(8,128)S(1)}, f32[128,512]{0,1:T(8,128)}, u32[]{:S(2)}, u32[]{:S(2)}) collective-permute-start(f32[128,512]{0,1:T(8,128)S(1)} %get-tuple-element.31), channel_id=1, source_target_pairs={{8,0},{16,8},{24,16},{9,1},{17,9},{25,17},{10,2},{18,10},{26,18},{... | collective-permute-start | bytes 786440 | tf_op jit(solution)/shard_map/ppermute | solution.py:18
  255.2 15.4 %collective-permute-start.10 = (f32[128,512]{0,1:T(8,128)S(1)}, f32[128,512]{0,1:T(8,128)}, u32[]{:S(2)}, u32[]{:S(2)}) collective-permute-start(f32[128,512]{0,1:T(8,128)S(1)} %get-tuple-element.30), channel_id=1, source_target_pairs={{0,1},{1,2},{2,3},{3,4},{4,5},{5,6},{6,7},{8,9},{9,10},{10,11},{11... | collective-permute-start | bytes 786440 | tf_op jit(solution)/shard_map/ppermute | solution.py:18
  260.9 11.4 %collective-permute-start.11 = (f32[128,512]{0,1:T(8,128)S(1)}, f32[128,512]{0,1:T(8,128)S(1)}, u32[]{:S(2)}, u32[]{:S(2)}) collective-permute-start(f32[128,512]{0,1:T(8,128)S(1)} %get-tuple-element.29), channel_id=1, source_target_pairs={{1,0},{2,1},{3,2},{4,3},{5,4},{6,5},{7,6},{9,8},{10,9},{11,10},{12... | collective-permute-start | bytes 786440 | tf_op jit(solution)/shard_map/ppermute | solution.py:18
  350.0 3.9 copy-start.8
